TPU v7x, 512 devices: a whole 4x8x8 slice. The times are simulated.
512 devices in a mesh: dp: 32 (over x, y), segment: 2 (over core), mp: 8 (over z).
Axes of the slice: x: 4, y: 8, z: 8, core: 2. Of those that a mesh axis runs over, the one named last changes fastest.
Arguments:
- frames: bfloat16 [2, 8192, 1280], P(None, ('dp', 'mp')), may hold values from -8 to 8
- dec_states: bfloat16 [2, 2048, 1280], P(None, 'dp'), may hold values from -8 to 8
- out_grad: bfloat16 [2, 2048, 1280], P(None, 'dp'), may hold values from -3 to 3
- frame_lengths: int32 [2, 32, 4], P(None, 'dp'), may hold values from 1 to 128, 256 in all within a row
- token_lengths: int32 [2, 32, 4], P(None, 'dp'), may hold values from 1 to 32, 64 in all within a row
- weights: bfloat16 [2, 4, 1024, 1280], P('segment', None, 'mp'), may hold values from -1 to 1
- norm_gains: float32 [3, 1280], replicated, may hold values from 0.25 to 1.75
- norm_biases: float32 [3, 1280], replicated, may hold values from -2 to 2
Outputs:
- gradient: float32 [2, 3, 1024, 1280], P('segment', None, 'mp')
Inputs may be any that keep to these rules, and one draw needn't show every extreme that they name: `frame_lengths`: the 4 utterance lengths of each micro-batch and group sum to 256. `token_lengths`: the 4 token counts of each micro-batch and group sum to 64.
All inputs are finite; a program needn't handle non-finite values.
Results may differ from a plain program's by a relative error of at most 0.04.
Values may be sent and summed in bfloat16 or wider, within the bound.
No kernel may reach another device: no remote copies, remote signals or barrier semaphores. Data moves between devices by JAX's collectives and lax.ppermute only.
A program may use at most 64 MiB of HBM per device.

v0:
```python
import math
import jax
import jax.numpy as jnp
from jax import lax
from jax.sharding import PartitionSpec as P

HS = 64
EPSILON = 1e-05
ROWS_DIMS = (((0,), (0,)), ((), ()))
FEAT_DIMS = (((1,), (1,)), ((), ()))


def partner(shard, axis, apart):
    return lax.ppermute(shard, axis, [(i, i ^ 1 << apart) for i in range(lax.axis_size(axis))])


def layer_norm(values, norm_gain, offset):
    center = values - jnp.mean(values, axis=-1, keepdims=True)
    variance = jnp.mean(center * center, axis=-1, keepdims=True)
    return center * lax.rsqrt(variance + EPSILON) * norm_gain + offset


def norm_backward(grad_out, values, norm_gain):
    center = values - jnp.mean(values, axis=-1, keepdims=True)
    variance = jnp.mean(center * center, axis=-1, keepdims=True)
    inverse = lax.rsqrt(variance + EPSILON)
    normed = center * inverse
    scaled = grad_out * norm_gain
    return inverse * (
        scaled
        - jnp.mean(scaled, axis=-1, keepdims=True)
        - normed * jnp.mean(scaled * normed, axis=-1, keepdims=True)
    )


def utterance_ids(lengths, row_count):
    bounds = jnp.cumsum(lengths, axis=1, dtype=jnp.int32)
    places = jnp.arange(row_count, dtype=jnp.int32)
    local_ids = jnp.sum((places[None, :, None] >= bounds[:, None, :]).astype(jnp.int32), axis=2)
    offsets = jnp.arange(lengths.shape[0], dtype=jnp.int32)[:, None] * lengths.shape[1]
    return (local_ids + offsets).reshape(-1)


def project(row_block, matrix):
    return lax.dot_general(row_block, matrix, FEAT_DIMS, preferred_element_type=jnp.float32).astype(
        jnp.bfloat16
    )


def outer_rows(left_rows, right_rows):
    return lax.dot_general(left_rows, right_rows, ROWS_DIMS, preferred_element_type=jnp.float32)


def split_heads(row_block):
    return row_block.reshape(row_block.shape[0], -1, HS)


def attend(queries, key_rows, value_rows, allowed):
    scaling = 1.0 / math.sqrt(HS)
    scores = (
        jnp.einsum(
            "qhd,khd->hqk",
            split_heads(queries),
            split_heads(key_rows),
            preferred_element_type=jnp.float32,
        )
        * scaling
    )
    scores = jnp.where(allowed[None], scores, -1e30)
    highest = jnp.max(scores, axis=-1, keepdims=True)
    raised = jnp.exp(scores - highest)
    attn_probs = raised / jnp.sum(raised, axis=-1, keepdims=True)
    context = jnp.einsum(
        "hqk,khd->qhd",
        attn_probs.astype(jnp.bfloat16),
        split_heads(value_rows),
        preferred_element_type=jnp.float32,
    )
    return (context.reshape(queries.shape[0], -1).astype(jnp.bfloat16), attn_probs)


def attend_backward(queries, key_rows, value_rows, attn_probs, grad_context):
    scaling = 1.0 / math.sqrt(HS)
    grad_heads = split_heads(grad_context)
    grad_probs = jnp.einsum(
        "qhd,khd->hqk", grad_heads, split_heads(value_rows), preferred_element_type=jnp.float32
    )
    grad_scores = (
        attn_probs * (grad_probs - jnp.sum(grad_probs * attn_probs, axis=-1, keepdims=True))
    ).astype(jnp.bfloat16)
    key_grad = (
        jnp.einsum(
            "hqk,qhd->khd", grad_scores, split_heads(queries), preferred_element_type=jnp.float32
        )
        * scaling
    )
    key_grad = key_grad.reshape(key_rows.shape[0], -1).astype(jnp.bfloat16)
    value_grad = jnp.einsum(
        "hqk,qhd->khd",
        attn_probs.astype(jnp.bfloat16),
        grad_heads,
        preferred_element_type=jnp.float32,
    )
    value_grad = value_grad.reshape(key_rows.shape[0], -1).astype(jnp.bfloat16)
    return (key_grad, value_grad)


def shards(
    frames, dec_states, out_grad, frame_lengths, token_lengths, weights, norm_gains, norm_biases
):
    is_encoder = lax.axis_index("segment") == 0
    matrices = weights[0]
    micro_count = frames.shape[0]
    shard_rows = frames.shape[1]
    features = frames.shape[2]
    head_cols = matrices.shape[1]
    head_count = head_cols // HS
    frame_count = shard_rows * lax.axis_size("mp")
    token_count = dec_states.shape[1]
    unit_count = micro_count // micro_count
    unit_rows = micro_count * frame_count
    received = jnp.zeros((micro_count, shard_rows, features), jnp.bfloat16)

    def empty_state():
        return (
            jnp.zeros((unit_rows, features), jnp.bfloat16),
            jnp.zeros((unit_rows, head_cols), jnp.bfloat16),
            jnp.zeros((unit_rows, head_cols), jnp.bfloat16),
            jnp.zeros((unit_rows, head_cols), jnp.bfloat16),
            jnp.zeros((unit_rows, head_cols), jnp.bfloat16),
            jnp.zeros((head_count, unit_rows, unit_rows), jnp.float32),
        )

    stored = {}
    totals = jnp.zeros((3, head_cols, features), jnp.float32)
    for moment in range(unit_count + 2):
        run_enc = moment < unit_count
        run_dec = 1 <= moment <= unit_count
        run_back = moment >= 2
        if run_enc:
            inputs = frames
        else:
            inputs = jnp.zeros((micro_count, shard_rows, features), jnp.bfloat16)
        enc_full, dec_full = (
            lax.all_gather(inputs, "mp", axis=1, tiled=True),
            lax.all_gather(received, "mp", axis=1, tiled=True),
        )

        def encoder_part():
            partial_value = jnp.zeros((unit_rows, features), jnp.float32)
            grad_step = jnp.zeros((3, head_cols, features), jnp.float32)
            saved_state = empty_state()
            if run_enc:
                lengths = frame_lengths[moment * micro_count : (moment + 1) * micro_count, 0]
                frame_ids = utterance_ids(lengths, frame_count)
                row_input = enc_full.reshape(unit_rows, features)
                normed = layer_norm(
                    row_input.astype(jnp.float32), norm_gains[0], norm_biases[0]
                ).astype(jnp.bfloat16)
                queries = project(normed, matrices[0])
                key_rows = project(normed, matrices[1])
                value_rows = project(normed, matrices[2])
                context, attn_probs = attend(
                    queries, key_rows, value_rows, frame_ids[:, None] == frame_ids[None, :]
                )
                partial_value = jnp.dot(context, matrices[3], preferred_element_type=jnp.float32)
                saved_state = (normed, queries, key_rows, value_rows, context, attn_probs)
            if run_back:
                normed_old, queries_old, keys_old, values_old, context_old, probs_old = stored[
                    moment - 2
                ]
                grad_rows = dec_full.reshape(unit_rows, features)
                out_weight_grad = outer_rows(context_old, grad_rows)
                grad_context = project(grad_rows, matrices[3])
                key_grad, value_grad = attend_backward(
                    queries_old, keys_old, values_old, probs_old, grad_context
                )
                grad_step = jnp.stack(
                    [
                        outer_rows(key_grad, normed_old),
                        outer_rows(value_grad, normed_old),
                        out_weight_grad,
                    ]
                )
            return (partial_value, grad_step, saved_state)

        def decoder_part():
            partial_value = jnp.zeros((unit_rows, features), jnp.float32)
            grad_step = jnp.zeros((3, head_cols, features), jnp.float32)
            if run_dec:
                batch_index = moment - 1
                first_micro = batch_index * micro_count
                frame_ids = utterance_ids(
                    frame_lengths[first_micro : first_micro + micro_count, 0], frame_count
                )
                token_ids = utterance_ids(
                    token_lengths[first_micro : first_micro + micro_count, 0], token_count
                )
                tokens = dec_states.reshape(micro_count * token_count, features)
                upstream = out_grad.reshape(micro_count * token_count, features)
                states_in = dec_full.reshape(unit_rows, features)
                normed = layer_norm(
                    states_in.astype(jnp.float32), norm_gains[2], norm_biases[2]
                ).astype(jnp.bfloat16)
                token_normed = layer_norm(
                    tokens.astype(jnp.float32), norm_gains[1], norm_biases[1]
                ).astype(jnp.bfloat16)
                queries = project(token_normed, matrices[0])
                key_rows = project(normed, matrices[1])
                value_rows = project(normed, matrices[2])
                context, attn_probs = attend(
                    queries, key_rows, value_rows, token_ids[:, None] == frame_ids[None, :]
                )
                grad_context = project(upstream, matrices[3])
                out_weight_grad = outer_rows(context, upstream)
                key_grad, value_grad = attend_backward(
                    queries, key_rows, value_rows, attn_probs, grad_context
                )
                grad_step = jnp.stack(
                    [outer_rows(key_grad, normed), outer_rows(value_grad, normed), out_weight_grad]
                )
                partial_value = jnp.dot(
                    key_grad, matrices[1], preferred_element_type=jnp.float32
                ) + jnp.dot(value_grad, matrices[2], preferred_element_type=jnp.float32)
            return (partial_value, grad_step, empty_state())

        partial_value, grad_step, saved_state = lax.cond(is_encoder, encoder_part, decoder_part)
        totals = totals + grad_step
        if run_enc:
            stored[moment] = saved_state
        if run_enc or run_dec:
            partial_value = partial_value.reshape(micro_count, frame_count, features)
            summed = lax.psum_scatter(
                partial_value.astype(jnp.bfloat16), "mp", scatter_dimension=1, tiled=True
            ).astype(jnp.float32)
            states_out = (inputs.astype(jnp.float32) + summed).astype(jnp.bfloat16)
            grads_out = norm_backward(summed, received.astype(jnp.float32), norm_gains[2]).astype(
                jnp.bfloat16
            )
            received = partner(jnp.where(is_encoder, states_out, grads_out), "segment", 0)
    gradient = lax.psum(totals.astype(jnp.bfloat16), "dp").astype(jnp.float32)
    return gradient[None]


def solution(mesh):
    placed = (
        P(None, ("dp", "mp"), None),
        P(None, "dp", None),
        P(None, "dp", None),
        P(None, "dp", None),
        P(None, "dp", None),
        P("segment", None, "mp", None),
        P(),
        P(),
    )
    return jax.shard_map(
        shards,
        mesh=mesh,
        in_specs=placed,
        out_specs=P("segment", None, "mp", None),
        check_vma=False,
    )
```

profile of v0, /device:TPU:16, one launch (start us, length us, event | category | flops | bytes accessed | tf_op | source)
XLA Modules:
  0.0 465.4 jit_solution(17567042108536954914)
XLA Ops:
  6.5 0.7 all-gather.4.cloned.1.call-update
  7.3 0.0 reduce-scatter.3.cloned.1.call-start
  7.3 49.3 %all-gather.4.cloned.1.call-done = bf16[2,256,1280]{2,1,0:T(8,128)(2,1)} async-done(((bf16[2,32,1280]{2,1,0:T(8,128)(2,1)}), bf16[2,256,1280]{2,1,0:T(8,128)(2,1)}) %all-gather.4.cloned.1.call-update) | async-done | bytes 1310736 | tf_op jit(solution)/shard_map/all_gather | solution.py:145
  56.6 21.9 %conditional.3 = (bf16[512,1280]{1,0:T(8,128)(2,1)}, bf16[512,1280]{1,0:T(8,128)(2,1)}, bf16[512,128]{0,1:T(8,128)(2,1)}, bf16[512,128]{0,1:T(8,128)(2,1)S(1)}, ...) conditional(s32[]{:T(128)} %convert_element_type.217, () %tuple.34, ...), branch_computations={%region_0.0_spmd, %region_1.8_spmd} | conditional | flops 820780032 | bytes 47561236 | solution.py:227
  56.7 0.9 slice_reduce_fusion
  57.5 1.6 convert_reduce_fusion
  59.1 0.6 fusion.28
  59.7 0.5 multiply_reduce_fusion.1
  60.2 0.6 fusion.29
  60.8 0.6 add_convert_fusion
  61.4 1.5 convolution_convert_fusion.5
  62.9 0.2 reduce_window_sum.17
  63.1 0.1 convert_reduce_fusion.1
  63.2 0.1 add_bitcast_fusion
  63.3 0.2 broadcast_compare_fusion
  63.5 2.2 convolution_convert_fusion.4
  65.7 1.5 convolution_convert_fusion.3
  67.2 3.8 fusion.87
  71.0 1.9 broadcast_divide_fusion
  72.9 1.3 convolution_convert_fusion.2
  74.2 2.7 fusion.15
  76.9 1.6 fusion.9
  78.5 0.0 copy-start.13
  78.5 0.0 reduce-scatter.3.cloned.1.call-update
  78.6 0.0 all-gather.6.cloned.1.call-start
  78.6 0.8 slice_reduce_fusion.6
  79.4 40.5 %reduce-scatter.3.cloned.1.call-done = bf16[2,32,1280]{2,1,0:T(8,128)(2,1)} async-done(((bf16[2,256,1280]{2,1,0:T(8,128)(2,1)}), bf16[2,32,1280]{2,1,0:T(8,128)(2,1)}) %reduce-scatter.3.cloned.1.call-update) | async-done | bytes 163856 | tf_op jit(solution)/shard_map/reduce_scatter | solution.py:233
  119.9 1.0 fusion.69
  121.0 1.1 fusion.86
  122.1 1.9 collective-permute-start
  124.0 1.4 collective-permute-done
  125.4 0.7 copy-done.4
  126.0 0.0 all-gather.6.cloned.1.call-update
  126.1 0.0 reduce-scatter.5.cloned.1.call-start
  126.1 40.7 %all-gather.6.cloned.1.call-done = bf16[2,256,1280]{2,1,0:T(8,128)(2,1)} async-done(((bf16[2,32,1280]{2,1,0:T(8,128)(2,1)}), bf16[2,256,1280]{2,1,0:T(8,128)(2,1)}) %all-gather.6.cloned.1.call-update) | async-done | bytes 1310736 | tf_op jit(solution)/shard_map/all_gather | solution.py:146
  166.8 2.6 conditional.4
  166.8 1.2 broadcast.393
  168.0 1.4 broadcast.394
  169.4 0.0 reduce-scatter.5.cloned.1.call-update
  169.5 0.2 all-gather.8.cloned.1.call-start
  169.7 1.0 convert_reduce_fusion.6
  170.7 1.1 fusion.78
  171.8 66.8 %reduce-scatter.5.cloned.1.call-done = bf16[2,32,1280]{2,1,0:T(8,128)(2,1)} async-done(((bf16[2,256,1280]{2,1,0:T(8,128)(2,1)}), bf16[2,32,1280]{2,1,0:T(8,128)(2,1)}) %reduce-scatter.5.cloned.1.call-update) | async-done | bytes 163856 | tf_op jit(solution)/shard_map/reduce_scatter | solution.py:233
  238.6 1.2 fusion.84
  239.9 1.2 fusion.85
  241.0 1.9 collective-permute-start.1
  243.0 1.4 collective-permute-done.1
  244.3 0.7 copy-done.11
  245.0 0.0 all-gather.8.cloned.1.call-update
  245.0 0.0 all-reduce.2.cloned.1.call-start
  245.1 40.9 %all-gather.8.cloned.1.call-done = bf16[2,256,1280]{2,1,0:T(8,128)(2,1)} async-done(((bf16[2,32,1280]{2,1,0:T(8,128)(2,1)}), bf16[2,256,1280]{2,1,0:T(8,128)(2,1)}) %all-gather.8.cloned.1.call-update) | async-done | bytes 1310736 | tf_op jit(solution)/shard_map/all_gather | solution.py:146
  285.9 9.2 %conditional.5 = (f32[3,128,1280]{2,1,0:T(8,128)S(1)}) conditional(s32[]{:T(128)} %convert_element_type.217, () %tuple.38, (bf16[2,256,1280]{2,1,0:T(8,128)(2,1)}, bf16[4,128,1280]{2,1,0:T(8,128)(2,1)}, bf16[512,128]{0,1:T(8,128)(2,1)S(1)}, f32[2,512,512]{1,2,0:T(8,128)S(1)}, bf16[512,128]{0,1:T(8,128)(2,1)}, ...), branch_computations={%region_29.30_spmd, %region_30.32_spmd} | conditional | flops 876805120 | bytes 28516388 | solution.py:227
  285.9 1.8 convolution_bitcast_fusion
  287.8 1.5 convolution_convert_fusion.1
  289.3 0.4 convolution_convert_fusion
  289.8 1.7 convolution_bitcast_fusion.1
  291.4 0.5 multiply_reduce_fusion
  291.9 1.4 fusion
  293.3 1.7 convolution_bitcast_fusion.2
  295.0 0.1 pad_maximum_fusion
  295.1 2.7 fusion.66
  297.9 0.0 all-reduce.2.cloned.1.call-update
  297.9 158.0 %all-reduce.2.cloned.1.call-done = bf16[1,3,128,1280]{3,2,1,0:T(8,128)(2,1)} async-done(((bf16[1,3,128,1280]{3,2,1,0:T(8,128)(2,1)}), bf16[1,3,128,1280]{3,2,1,0:T(8,128)(2,1)}) %all-reduce.2.cloned.1.call-update) | async-done | bytes 983056 | tf_op jit(solution)/shard_map/psum | solution.py:241
  455.9 2.6 broadcast_in_dim.37
  (39 shorter events, 0.1 us)
Async XLA Ops:
  6.5 50.1 %all-gather.4.cloned.1.call-start = ((), (), s32[]{:S(2)}) async-start(), calls=%async_computation.2 | async-start | bytes 1474560 | tf_op jit(solution)/shard_map/all_gather | solution.py:145
  7.3 112.6 %reduce-scatter.3.cloned.1.call-start = ((), (), s32[]{:S(2)}) async-start(), calls=%async_computation.3 | async-start | bytes 1474560 | tf_op jit(solution)/shard_map/reduce_scatter | solution.py:233
  56.6 3.1 copy-start.2
  60.8 2.1 copy-start.17
  62.9 10.0 %copy-start.8 = (bf16[512,128]{0,1:T(8,128)(2,1)}, bf16[512,128]{0,1:T(8,128)(2,1)S(1)}, u32[]{:S(2)}) copy-start(bf16[512,128]{0,1:T(8,128)(2,1)S(1)} %convolution_convert_fusion.5) | copy-start | bytes 393220 | tf_op jit(solution)/shard_map/cond
  72.9 4.0 copy-start
  72.9 3.9 copy-start.15
  72.9 4.0 copy-start.14
  74.2 4.3 copy-start.9
  76.8 1.7 copy-start.1
  78.5 88.3 %copy-start.6 = (bf16[2,64,1280]{2,1,0:T(8,128)(2,1)S(1)}, bf16[2,64,1280]{2,1,0:T(8,128)(2,1)}, u32[]{:S(2)}) copy-start(bf16[2,64,1280]{2,1,0:T(8,128)(2,1)} %param.15) | copy-start | bytes 983044
  78.5 88.3 %copy-start.12 = (f32[3,1280]{1,0:T(4,128)S(1)}, f32[3,1280]{1,0:T(4,128)}, u32[]{:S(2)}) copy-start(f32[3,1280]{1,0:T(4,128)} %param.20) | copy-start | bytes 46084
  78.5 88.3 %copy-start.13 = (f32[3,1280]{1,0:T(4,128)S(1)}, f32[3,1280]{1,0:T(4,128)}, u32[]{:S(2)}) copy-start(f32[3,1280]{1,0:T(4,128)} %param.21) | copy-start | bytes 46084
  78.5 88.3 %copy-start.16 = (s32[2,1,4]{2,1,0:T(1,128)S(1)}, s32[2,1,4]{2,1,0:T(1,128)}, u32[]{:S(2)}) copy-start(s32[2,1,4]{2,1,0:T(1,128)} %param.17) | copy-start | bytes 100
  78.6 88.2 %all-gather.6.cloned.1.call-start = ((), (), s32[]{:S(2)}) async-start(), calls=%async_computation.4 | async-start | bytes 1474560 | tf_op jit(solution)/shard_map/all_gather | solution.py:146
  122.1 3.3 collective-permute-start
  125.4 0.7 copy-start.4
  126.1 112.6 %reduce-scatter.5.cloned.1.call-start = ((), (), s32[]{:S(2)}) async-start(), calls=%async_computation.5 | async-start | bytes 1474560 | tf_op jit(solution)/shard_map/reduce_scatter | solution.py:233
  169.4 70.4 %copy-start.5 = (bf16[2,32,1280]{2,1,0:T(8,128)(2,1)S(1)}, bf16[2,32,1280]{2,1,0:T(8,128)(2,1)}, u32[]{:S(2)}) copy-start(bf16[2,32,1280]{2,1,0:T(8,128)(2,1)} %copy-done.4) | copy-start | bytes 491524
  169.5 116.5 %all-gather.8.cloned.1.call-start = ((), (), s32[]{:S(2)}) async-start(), calls=%async_computation.6 | async-start | bytes 1474560 | tf_op jit(solution)/shard_map/all_gather | solution.py:146
  241.0 3.3 collective-permute-start.1
  244.3 0.7 copy-start.11
  245.0 210.9 %all-reduce.2.cloned.1.call-start = ((), (), s32[]{:S(2)}) async-start(), calls=%async_computation.7 | async-start | bytes 1966080 | tf_op jit(solution)/shard_map/psum | solution.py:241
  285.9 1.8 copy-start.7
Sparse Core Ops, SparseCore 0:
  9.4 47.1 all-gather.3
  78.7 41.1 reduce-scatter.2
  126.2 40.5 all-gather.5
  169.6 68.9 reduce-scatter.4
  245.1 40.7 all-gather.7
  298.0 157.8 all-reduce.1
where the time goes:
time: 466 us; the launch traced here: 465 us
  waiting for transfers between devices  400 us (86%)
  matrix products  21.9 us (5%)
  other arithmetic  20.1 us (4%)
  between operations  13.6 us (3%)
  local copies, waits for them, and re-layouts  5.66 us (1%)
    psum x1, waiting for transfers between devices, shards(): gradient = lax.psum(totals.astype(jnp.bfloat16), 'dp').astype(jnp.float32)  158 us
    reduce_scatter x2, waiting for transfers between devices, shards(): lax.psum_scatter(partial_value.astype(jnp.bfloat16), 'mp', scatter_dimens...  107 us
    all_gather x2, waiting for transfers between devices, shards(): lax.all_gather(received, 'mp', axis=1, tiled=True)  81.6 us
    all_gather x1, waiting for transfers between devices, shards(): lax.all_gather(inputs, 'mp', axis=1, tiled=True)  49.3 us
  transfers between devices with their start and end apart: 8, of which 8 were waited for; matrix products, arithmetic and copies ran while one was open for 1% of the time, Pallas kernels for 0%

commit v1 on v0

--- a/solution.py
+++ b/solution.py
@@ -3,11 +3,16 @@
 import jax.numpy as jnp
 from jax import lax
 from jax.sharding import PartitionSpec as P
+from jax.lax import all_gather
 
 HS = 64
 EPSILON = 1e-05
 ROWS_DIMS = (((0,), (0,)), ((), ()))
 FEAT_DIMS = (((1,), (1,)), ((), ()))
+
+
+def shape_forms(body):
+    return jnp.sum(all_gather(body, "dp"), axis=0)
 
 
 def partner(shard, axis, apart):
@@ -238,7 +243,7 @@
                 jnp.bfloat16
             )
             received = partner(jnp.where(is_encoder, states_out, grads_out), "segment", 0)
-    gradient = lax.psum(totals.astype(jnp.bfloat16), "dp").astype(jnp.float32)
+    gradient = shape_forms(totals.astype(jnp.bfloat16)).astype(jnp.float32)
     return gradient[None]
 
 

time: 466 us -> 522 us (1.12)
  the two profiles are of different devices: /device:TPU:16 before, /device:TPU:1 now
where the time goes in v1:
time: 522 us; the launch traced here: 521 us
  waiting for transfers between devices  450 us (86%)
  other arithmetic  24.2 us (5%)
  starting transfers between devices  13.9 us (3%)
  between operations  13.6 us (3%)
  local copies, waits for them, and re-layouts  11 us (2%)
  matrix products  8.14 us (2%)
    all_gather x1, waiting for transfers between devices, shape_forms(): return jnp.sum(all_gather(body, 'dp'), axis=0)  239 us
    reduce_scatter x2, waiting for transfers between devices, shards(): lax.psum_scatter(partial_value.astype(jnp.bfloat16), 'mp', scatter_dimens...  90.3 us
    all_gather x2, waiting for transfers between devices, shards(): lax.all_gather(received, 'mp', axis=1, tiled=True)  72.2 us
    all_gather x1, waiting for transfers between devices, shards(): lax.all_gather(inputs, 'mp', axis=1, tiled=True)  45.8 us
    ppermute x2, starting transfers between devices, partner(): lax.ppermute(shard, axis, [(i, i ^ 1 << apart) for i in range(lax.axis_si...  13.5 us
    reduce_sum x1, other arithmetic, shape_forms(): return jnp.sum(all_gather(body, 'dp'), axis=0)  11.1 us
  transfers between devices with their start and end apart: 8, of which 8 were waited for; matrix products, arithmetic and copies ran while one was open for 0% of the time, Pallas kernels for 0%

profile of v1, /device:TPU:1, one launch (start us, length us, event | category | flops | bytes accessed | tf_op | source)
XLA Modules:
  0.0 521.0 jit_solution(14301972151272070039)
XLA Ops:
  6.5 0.7 all-gather.6.cloned.1.call-update
  7.3 45.8 %all-gather.6.cloned.1.call-done = bf16[2,256,1280]{2,1,0:T(8,128)(2,1)} async-done(((bf16[2,32,1280]{2,1,0:T(8,128)(2,1)}), bf16[2,256,1280]{2,1,0:T(8,128)(2,1)}) %all-gather.6.cloned.1.call-update) | async-done | bytes 1310736 | tf_op jit(solution)/shard_map/all_gather | solution.py:150
  53.1 4.8 conditional.3
  53.1 1.1 broadcast.378
  54.3 1.6 broadcast.381
  55.9 0.6 broadcast.380.clone.1
  56.5 0.7 broadcast.380.clone
  57.2 0.7 broadcast.380
  57.8 0.1 broadcast.379
  58.1 1.3 slice_reduce_fusion.6
  59.4 53.9 %reduce-scatter.3.cloned.1.call-done = bf16[2,32,1280]{2,1,0:T(8,128)(2,1)} async-done(((bf16[2,256,1280]{2,1,0:T(8,128)(2,1)}), bf16[2,32,1280]{2,1,0:T(8,128)(2,1)}) %reduce-scatter.3.cloned.1.call-update) | async-done | bytes 163856 | tf_op jit(solution)/shard_map/reduce_scatter | solution.py:238
  113.3 1.0 fusion.68
  114.4 1.1 fusion.85
  115.5 6.9 %collective-permute-start = (bf16[2,32,1280]{2,1,0:T(8,128)(2,1)S(1)}, bf16[2,32,1280]{2,1,0:T(8,128)(2,1)S(1)}, u32[]{:S(2)}, u32[]{:S(2)}) collective-permute-start(bf16[2,32,1280]{2,1,0:T(8,128)(2,1)S(1)} %fusion.85), channel_id=1, source_target_pairs={{0,8},{8,0},{1,9},{9,1},{2,10},{10,2},{3,11},{11,3},{4,12},{12,4},... | collective-permute-start | bytes 491528 | tf_op jit(solution)/shard_map/ppermute | solution.py:19
  122.4 1.0 collective-permute-done
  123.4 0.7 copy-done.4
  124.2 36.1 %all-gather.8.cloned.1.call-done = bf16[2,256,1280]{2,1,0:T(8,128)(2,1)} async-done(((bf16[2,32,1280]{2,1,0:T(8,128)(2,1)}), bf16[2,256,1280]{2,1,0:T(8,128)(2,1)}) %all-gather.8.cloned.1.call-update) | async-done | bytes 1310736 | tf_op jit(solution)/shard_map/all_gather | solution.py:151
  160.3 14.6 %conditional.4 = (bf16[512,1280]{1,0:T(8,128)(2,1)}, f32[3,128,1280]{2,1,0:T(8,128)S(1)}) conditional(s32[]{:T(128)} %convert_element_type.231, (bf16[2,64,1280]{2,1,0:T(8,128)(2,1)S(1)}, f32[3,1280]{1,0:T(4,128)S(1)}, f32[3,1280]{1,0:T(4,128)S(1)}, bf16[4,128,1280]{2,1,0:T(8,128)(2,1)}, s32[2,1,4]{2,1,0:T(1,128)S(1)}, ...), branch_computations={%region_11.23_spmd, %region_23.24_spmd} | conditional | flops 1282403072 | bytes 51815376 | solution.py:232
  160.3 0.2 reduce_window_sum.21
  160.5 0.1 convert_reduce_fusion.4
  160.7 0.2 reduce_window_sum.19
  160.8 0.1 convert_reduce_fusion.5
  161.0 0.1 add.142
  161.1 0.1 convert_reduce_fusion.3
  161.2 0.2 fusion.43
  161.5 1.6 convert_reduce_fusion.2
  163.1 0.5 fusion.33
  163.6 0.2 convolution_convert_fusion.9
  163.9 0.6 fusion.36
  164.4 0.1 broadcast_compare_fusion.1
  164.6 0.6 convolution_convert_fusion.7
  165.1 0.6 convolution_convert_fusion.8
  165.7 0.3 fusion.46
  166.0 0.2 convolution_convert_fusion.10
  166.2 0.4 fusion.87
  166.7 1.1 multiply_reduce_fusion.2
  167.7 0.7 convolution_convert_fusion.11
  168.4 0.3 copy-done.23
  168.8 0.7 fusion.40
  169.5 0.6 convolution_convert_fusion.6
  170.1 0.2 convolution_bitcast_fusion.3
  170.3 0.3 convolution_bitcast_fusion.5
  170.7 0.3 convolution_bitcast_fusion.4
  171.1 0.1 pad_maximum_fusion.1
  171.3 1.1 copy-done.10
  172.4 0.5 fusion.50
  172.9 0.4 copy-done.14
  173.3 1.6 convolution_add_fusion
  174.9 0.2 all-gather.10.cloned.1.call-start
  175.2 0.1 convert_reduce_fusion.6
  175.3 0.2 fusion.77
  175.5 36.5 %reduce-scatter.5.cloned.1.call-done = bf16[2,32,1280]{2,1,0:T(8,128)(2,1)} async-done(((bf16[2,256,1280]{2,1,0:T(8,128)(2,1)}), bf16[2,32,1280]{2,1,0:T(8,128)(2,1)}) %reduce-scatter.5.cloned.1.call-update) | async-done | bytes 163856 | tf_op jit(solution)/shard_map/reduce_scatter | solution.py:238
  212.0 1.1 fusion.83
  213.1 1.2 fusion.84
  214.3 6.6 %collective-permute-start.1 = (bf16[2,32,1280]{2,1,0:T(8,128)(2,1)S(1)}, bf16[2,32,1280]{2,1,0:T(8,128)(2,1)S(1)}, u32[]{:S(2)}, u32[]{:S(2)}) collective-permute-start(bf16[2,32,1280]{2,1,0:T(8,128)(2,1)S(1)} %fusion.84), channel_id=1, source_target_pairs={{0,8},{8,0},{1,9},{9,1},{2,10},{10,2},{3,11},{11,3},{4,12},{12,4},... | collective-permute-start | bytes 491528 | tf_op jit(solution)/shard_map/ppermute | solution.py:19
  220.9 1.0 collective-permute-done.1
  221.9 0.7 copy-done.18
  222.7 36.1 %all-gather.10.cloned.1.call-done = bf16[2,256,1280]{2,1,0:T(8,128)(2,1)} async-done(((bf16[2,32,1280]{2,1,0:T(8,128)(2,1)}), bf16[2,256,1280]{2,1,0:T(8,128)(2,1)}) %all-gather.10.cloned.1.call-update) | async-done | bytes 1310736 | tf_op jit(solution)/shard_map/all_gather | solution.py:151
  258.8 1.4 conditional.5
  258.8 1.4 broadcast.395
  260.2 2.7 add_convert_fusion.1
  263.0 238.8 %all-gather.12.cloned.1.call-done = bf16[96,128,1280]{2,1,0:T(8,128)(2,1)} async-done(((bf16[3,128,1280]{2,1,0:T(8,128)(2,1)}), bf16[96,128,1280]{2,1,0:T(8,128)(2,1)}) %all-gather.12.cloned.1.call-update) | async-done | bytes 31457296 | tf_op jit(solution)/shard_map/all_gather | solution.py:15
  501.7 11.1 %reduce_sum.199 = bf16[3,128,1280]{2,1,0:T(8,128)(2,1)S(1)} reduce(bf16[32,3,128,1280]{3,2,1,0:T(8,128)(2,1)} %bitcast.154, bf16[]{:T(256)} %constant.111.clone.1), dimensions={0}, to_apply=%region_32.33 | reduce | flops 15237120 | bytes 32440322 | tf_op jit(solution)/shard_map/reduce_sum | solution.py:15
  512.8 1.4 bitcast_convert_fusion
  (57 shorter events, 0.6 us)
Async XLA Ops:
  6.5 46.6 %all-gather.6.cloned.1.call-start = ((), (), s32[]{:S(2)}) async-start(), calls=%async_computation.2 | async-start | bytes 1474560 | tf_op jit(solution)/shard_map/all_gather | solution.py:150
  7.3 106.1 %reduce-scatter.3.cloned.1.call-start = ((), (), s32[]{:S(2)}) async-start(), calls=%async_computation.3 | async-start | bytes 1474560 | tf_op jit(solution)/shard_map/reduce_scatter | solution.py:238
  57.9 102.3 %copy-start.2 = (bf16[512,1280]{1,0:T(8,128)(2,1)}, bf16[512,1280]{1,0:T(8,128)(2,1)S(1)}, u32[]{:S(2)}) copy-start(bf16[512,1280]{1,0:T(8,128)(2,1)S(1)} %get-tuple-element.111) | copy-start | bytes 3932164
  57.9 102.3 %copy-start.6 = (bf16[2,64,1280]{2,1,0:T(8,128)(2,1)S(1)}, bf16[2,64,1280]{2,1,0:T(8,128)(2,1)}, u32[]{:S(2)}) copy-start(bf16[2,64,1280]{2,1,0:T(8,128)(2,1)} %param.15) | copy-start | bytes 983044
  58.0 102.3 %copy-start.17 = (bf16[2,64,1280]{2,1,0:T(8,128)(2,1)S(1)}, bf16[2,64,1280]{2,1,0:T(8,128)(2,1)}, u32[]{:S(2)}) copy-start(bf16[2,64,1280]{2,1,0:T(8,128)(2,1)} %param.16) | copy-start | bytes 983044
  58.0 102.3 %copy-start.19 = (f32[3,1280]{1,0:T(4,128)S(1)}, f32[3,1280]{1,0:T(4,128)}, u32[]{:S(2)}) copy-start(f32[3,1280]{1,0:T(4,128)} %param.20) | copy-start | bytes 46084
  58.0 102.2 %copy-start.20 = (f32[3,1280]{1,0:T(4,128)S(1)}, f32[3,1280]{1,0:T(4,128)}, u32[]{:S(2)}) copy-start(f32[3,1280]{1,0:T(4,128)} %param.21) | copy-start | bytes 46084
  58.0 102.2 %copy-start.21 = (s32[2,1,4]{2,1,0:T(1,128)S(1)}, s32[2,1,4]{2,1,0:T(1,128)}, u32[]{:S(2)}) copy-start(s32[2,1,4]{2,1,0:T(1,128)} %param.17) | copy-start | bytes 100
  58.0 102.2 %copy-start.22 = (s32[2,1,4]{2,1,0:T(1,128)S(1)}, s32[2,1,4]{2,1,0:T(1,128)}, u32[]{:S(2)}) copy-start(s32[2,1,4]{2,1,0:T(1,128)} %param.18) | copy-start | bytes 100
  58.0 102.2 %all-gather.8.cloned.1.call-start = ((), (), s32[]{:S(2)}) async-start(), calls=%async_computation.4 | async-start | bytes 1474560 | tf_op jit(solution)/shard_map/all_gather | solution.py:151
  115.5 7.9 %collective-permute-start = (bf16[2,32,1280]{2,1,0:T(8,128)(2,1)S(1)}, bf16[2,32,1280]{2,1,0:T(8,128)(2,1)S(1)}, u32[]{:S(2)}, u32[]{:S(2)}) collective-permute-start(bf16[2,32,1280]{2,1,0:T(8,128)(2,1)S(1)} %fusion.85), channel_id=1, source_target_pairs={{0,8},{8,0},{1,9},{9,1},{2,10},{10,2},{3,11},{11,3},{4,12},{12,4},... | collective-permute-start | bytes 491528 | tf_op jit(solution)/shard_map/ppermute | solution.py:19
  123.4 0.7 copy-start.4
  124.1 87.8 %reduce-scatter.5.cloned.1.call-start = ((), (), s32[]{:S(2)}) async-start(), calls=%async_computation.5 | async-start | bytes 1474560 | tf_op jit(solution)/shard_map/reduce_scatter | solution.py:238
  160.3 14.9 %copy-start.5 = (bf16[2,32,1280]{2,1,0:T(8,128)(2,1)S(1)}, bf16[2,32,1280]{2,1,0:T(8,128)(2,1)}, u32[]{:S(2)}) copy-start(bf16[2,32,1280]{2,1,0:T(8,128)(2,1)} %copy-done.4) | copy-start | bytes 491524
  160.3 2.8 copy-start.1
  161.1 2.5 copy-start.9
  167.7 1.0 copy-start.23
  169.5 1.2 copy-start.11
  170.1 0.6 copy-start.13
  171.1 1.3 copy-start.10
  171.1 1.3 copy-start.12
  172.4 0.9 copy-start.14
  174.9 83.9 %copy-start.3 = (bf16[512,1280]{1,0:T(8,128)(2,1)S(1)}, bf16[512,1280]{1,0:T(8,128)(2,1)}, u32[]{:S(2)}) copy-start(bf16[512,1280]{1,0:T(8,128)(2,1)} %copy-done.2) | copy-start | bytes 3932164
  174.9 83.8 %all-gather.10.cloned.1.call-start = ((), (), s32[]{:S(2)}) async-start(), calls=%async_computation.6 | async-start | bytes 1474560 | tf_op jit(solution)/shard_map/all_gather | solution.py:151
  214.3 7.7 %collective-permute-start.1 = (bf16[2,32,1280]{2,1,0:T(8,128)(2,1)S(1)}, bf16[2,32,1280]{2,1,0:T(8,128)(2,1)S(1)}, u32[]{:S(2)}, u32[]{:S(2)}) collective-permute-start(bf16[2,32,1280]{2,1,0:T(8,128)(2,1)S(1)} %fusion.84), channel_id=1, source_target_pairs={{0,8},{8,0},{1,9},{9,1},{2,10},{10,2},{3,11},{11,3},{4,12},{12,4},... | collective-permute-start | bytes 491528 | tf_op jit(solution)/shard_map/ppermute | solution.py:19
  221.9 0.7 copy-start.18
  222.6 279.1 %all-gather.12.cloned.1.call-start = ((), (), s32[]{:S(2)}) async-start(), calls=%async_computation.7 | async-start | bytes 32440320 | tf_op jit(solution)/shard_map/all_gather | solution.py:15
Sparse Core Ops, SparseCore 0:
  9.4 43.6 all-gather.5
  58.2 55.1 reduce-scatter.2
  124.2 35.9 all-gather.7
  175.1 36.8 reduce-scatter.4
  222.7 35.9 all-gather.9
  263.1 238.5 all-gather.11
